TPU v7x, 32 devices: a whole 2x2x4 slice. The times are simulated.
32 devices in a mesh: inner: 4 (over y, x), outer: 8 (over z, core).
Axes of the slice: x: 2, y: 2, z: 4, core: 2. Of those that a mesh axis runs over, the one named last changes fastest.
Arguments:
- jac: float32 [512, 256, 256], P(('outer', 'inner')), may hold values from -0.5 to 1
- obs: float32 [512, 256], P(('outer', 'inner')), may hold values from -6 to 6
- gain_filter: float32 [256], replicated, may hold values from 0 to 0.1
- gain_smooth: float32 [256, 256], replicated, may hold values from -0.5 to 1
- init_mean: float32 [256], replicated, may hold values from -6 to 6
Outputs:
- filtered: float32 [512, 256], P(('outer', 'inner'))
- smoothed: float32 [512, 256], P(('outer', 'inner'))
All inputs are finite; a program needn't handle non-finite values.
Results may differ from a plain program's by a relative error of at most 0.0003.
Values sent between devices are 32-bit elements; how exact they have to be, the bound alone decides.
A program may use at most 64 MiB of HBM per device.

v0:
```python
import jax
import jax.numpy as jnp
from jax import lax
from jax.sharding import PartitionSpec as P

HIGHEST = lax.Precision.HIGHEST


def entering(part, axis, combine, identity):
    place = lax.axis_index(axis)
    gathered = lax.all_gather(part, axis)
    state = jnp.zeros_like(part) + jnp.asarray(identity, part.dtype)

    def one(turn, state):
        return combine(state, lax.dynamic_index_in_dim(gathered, turn, 0, False))

    return lax.fori_loop(0, place, one, state)


def last_row(state_width):
    return (jnp.arange(state_width + 1) == state_width).astype(jnp.float32)[:, None]


def identity_map(state_width):
    return jnp.concatenate(
        [jnp.eye(state_width, dtype=jnp.float32), jnp.zeros((1, state_width), jnp.float32)], 0
    )


def compose(earlier, later):
    state_width = later.shape[1]
    product = jnp.dot(earlier, later[:state_width], precision=HIGHEST)
    return product + last_row(state_width) * later[state_width][None, :]


def advance(packed, state):
    state_width = packed.shape[1]
    return jnp.dot(state, packed[:state_width], precision=HIGHEST) + packed[state_width]


def raise_power(factor, count):
    result = jnp.eye(factor.shape[0], dtype=jnp.float32)
    square = factor
    while count > 0:
        if count % 2 == 1:
            result = jnp.dot(result, square, precision=HIGHEST)
        count = count // 2
        if count > 0:
            square = jnp.dot(square, square, precision=HIGHEST)
    return result


def incoming_state(own_map, boundary):
    state_width = own_map.shape[1]
    identity = identity_map(state_width)
    inner_count = lax.axis_size("inner")
    inner_here = lax.axis_index("inner")
    gathered = lax.all_gather(own_map[None], "inner", axis=0, tiled=True)

    def absorb(running, inputs):
        before, group_total = running
        segment, position = inputs
        group_total = compose(group_total, segment)
        taken = position < inner_here
        before = jnp.where(taken, group_total, before)
        return ((before, group_total), None)

    (seg_before, group_total), _ = lax.scan(
        absorb,
        (identity, identity),
        (gathered, jnp.arange(inner_count, dtype=jnp.int32)),
        reverse=False,
    )
    group_before = entering(group_total, "outer", compose, identity)
    group_state = advance(group_before, boundary)
    return advance(seg_before, group_state)


def entering_backward(offset_sum, step_power):
    inner_count = lax.axis_size("inner")
    inner_here = lax.axis_index("inner")
    outer_count = lax.axis_size("outer")
    outer_here = lax.axis_index("outer")
    zero_state = jnp.zeros_like(offset_sum)
    seg_offsets = lax.all_gather(offset_sum[None], "inner", axis=0, tiled=True)

    def run_affine(power, here):

        def turn(running, inputs):
            state, caught = running
            offset, position = inputs
            caught = jnp.where(position == here, state, caught)
            state = jnp.dot(state, power, precision=HIGHEST) + offset
            return ((state, caught), None)

        return turn

    (group_offset, _), _ = lax.scan(
        run_affine(step_power, inner_here),
        (zero_state, zero_state),
        (seg_offsets, jnp.arange(inner_count, dtype=jnp.int32)),
        reverse=True,
    )
    group_power = raise_power(step_power, inner_count)
    group_offsets = lax.all_gather(group_offset[None], "outer", axis=0, tiled=True)
    (_, group_state), _ = lax.scan(
        run_affine(group_power, outer_here),
        (zero_state, zero_state),
        (group_offsets, jnp.arange(outer_count, dtype=jnp.int32)),
        reverse=True,
    )
    (_, device_state), _ = lax.scan(
        run_affine(step_power, inner_here),
        (group_state, group_state),
        (seg_offsets, jnp.arange(inner_count, dtype=jnp.int32)),
        reverse=True,
    )
    return device_state


def shards(jac, obs, gain_filter, gain_smooth, init_mean):
    state_width = jac.shape[1]
    step_count = jac.shape[0]
    retain = 1.0 - gain_filter
    bottom = last_row(state_width)

    def compose_forward(packed, inputs):
        step_matrix, measured = inputs
        moved = (
            lax.dot_general(packed, step_matrix, (((1,), (1,)), ((), ())), precision=HIGHEST)
            * retain[None, :]
        )
        return (moved + bottom * (gain_filter * measured)[None, :], None)

    forward_map, _ = lax.scan(compose_forward, identity_map(state_width), (jac, obs))
    start_state = incoming_state(forward_map, init_mean)

    def forward(state, inputs):
        step_matrix, measured = inputs
        predicted = jnp.dot(step_matrix, state, precision=HIGHEST)
        updated = predicted + gain_filter * (measured - predicted)
        return (updated, (predicted, updated))

    _, (predicted_all, filtered_all) = lax.scan(forward, start_state, (jac, obs))
    correction = filtered_all - predicted_all

    def backward(state, term):
        renewed = jnp.dot(gain_smooth, state, precision=HIGHEST) + term
        return (renewed, renewed)

    zero_state = jnp.zeros((state_width,), jnp.float32)
    offset_sum, _ = lax.scan(backward, zero_state, correction, reverse=True)
    step_power = raise_power(gain_smooth.T, step_count)
    after_state = entering_backward(offset_sum, step_power)
    _, back_states = lax.scan(backward, after_state, correction, reverse=True)
    return (filtered_all, predicted_all + back_states)


def solution(mesh):
    return jax.shard_map(
        shards,
        mesh=mesh,
        in_specs=(P(("outer", "inner"), None, None), P(("outer", "inner"), None), P(), P(), P()),
        out_specs=(P(("outer", "inner"), None), P(("outer", "inner"), None)),
        check_vma=False,
    )
```

profile of v0, /device:TPU:0, one launch (start us, length us, event | category | flops | bytes accessed | tf_op | source)
XLA Modules:
  0.0 221.8 jit_solution(6826046817942252627)
XLA Ops:
  8.0 34.7 %while.131 = (s32[]{:T(128)}, f32[257,256]{1,0:T(8,128)S(1)}, f32[16,256,256]{2,1,0:T(8,128)}, f32[256]{0:T(256)S(1)}, f32[256]{0:T(256)}, /*index=5*/f32[16,256]{1,0:T(8,128)}, s32[]{:T(128)}) while((s32[]{:T(128)}, f32[257,256]{1,0:T(8,128)S(1)}, f32[16,256,256]{2,1,0:T(8,128)}, f32[256]{0:T(256)S(1)}, f32[256]{0:T(256)}, ...), condition=%wide.region_1.2_spmd.clone, body=%wide.region_0.1_spmd.clone.sunk | while | flops 202311168 | bytes 1322585 | solution.py:135
  8.8 1.4 fusion.109
  10.9 1.4 fusion.109
  13.1 1.4 fusion.109
  15.3 1.4 fusion.109
  17.4 1.4 fusion.109
  19.6 1.4 fusion.109
  21.8 1.4 fusion.109
  23.9 1.4 fusion.109
  26.1 1.4 fusion.109
  28.3 1.4 fusion.109
  30.5 1.4 fusion.109
  32.6 1.4 fusion.109
  34.8 1.4 fusion.109
  37.0 1.4 fusion.109
  39.1 1.4 fusion.109
  41.3 1.4 fusion.109
  43.5 29.5 %all-gather.11.cloned.1.call-done = f32[4,257,256]{2,1,0:T(8,128)} async-done(((f32[1,257,256]{2,1,0:T(8,128)}), f32[4,257,256]{2,1,0:T(8,128)}) %all-gather.11.cloned.1.call-update) | async-done | bytes 1052688 | tf_op jit(solution)/shard_map/all_gather | solution.py:58
  73.1 14.0 %while.126 = (s32[]{:T(128)}, f32[257,256]{1,0:T(8,128)S(1)}, f32[257,256]{1,0:T(8,128)S(1)}, s32[4]{0:T(128)S(1)}, s32[]{:T(128)}, /*index=5*/f32[4,257,256]{2,1,0:T(8,128)}, s32[]{:T(128)}, s32[]{:T(128)}, s32[]{}) while((s32[]{:T(128)}, f32[257,256]{1,0:T(8,128)S(1)}, f32[257,256]{1,0:T(8,128)S(1)}, s32[4]{0:T(128)S(1)}, s32[]{:T(128)}, ...), condition=%wide.region_3.4_spmd, body=%wide.region_2.3_spmd.sunk | while | flops 202310912 | bytes 1846927 | solution.py:68
  75.1 1.5 broadcast_select_fusion.9
  78.6 1.5 broadcast_select_fusion.9
  82.1 1.5 broadcast_select_fusion.9
  85.6 1.5 broadcast_select_fusion.9
  91.0 26.7 %all-gather.13.cloned.1.call-done = f32[8,257,256]{2,1,0:T(8,128)} async-done(((f32[1,257,256]{2,1,0:T(8,128)}), f32[8,257,256]{2,1,0:T(8,128)}) %all-gather.13.cloned.1.call-update) | async-done | bytes 2105360 | tf_op jit(solution)/shard_map/all_gather | solution.py:11
  118.3 33.3 %while.128 = (s32[]{:T(128)}, f32[256]{0:T(256)S(1)}, f32[16,256]{1,0:T(8,128)S(1)}, f32[16,256]{1,0:T(8,128)S(1)}, f32[16,256,256]{2,1,0:T(8,128)}, /*index=5*/...) while((s32[]{:T(128)}, f32[256]{0:T(256)S(1)}, f32[16,256]{1,0:T(8,128)S(1)}, ...), condition=%wide.region_7.8_spmd, body=%wide.region_6.7_spmd.sunk | while | flops 787202 | bytes 275049 | solution.py:144
  118.3 1.2 fusion.99
  120.4 1.2 fusion.99
  122.5 1.2 fusion.99
  124.6 1.2 fusion.99
  126.6 1.2 fusion.99
  128.7 1.2 fusion.99
  130.8 1.2 fusion.99
  132.9 1.2 fusion.99
  135.0 1.2 fusion.99
  137.1 1.2 fusion.99
  139.1 1.2 fusion.99
  141.2 1.2 fusion.99
  143.3 1.2 fusion.99
  145.4 1.2 fusion.99
  147.5 1.2 fusion.99
  149.5 1.2 fusion.99
  151.6 6.1 %while.132 = (s32[]{:T(128)}, f32[256]{0:T(256)S(1)}, f32[256,256]{1,0:T(8,128)S(1)}, f32[16,256]{1,0:T(8,128)S(1)}, s32[]{:T(128)}, /*index=5*/s32[]{:T(128)}, s32[]{:T(128)}) while((s32[]{:T(128)}, f32[256]{0:T(256)S(1)}, f32[256,256]{1,0:T(8,128)S(1)}, f32[16,256]{1,0:T(8,128)S(1)}, s32[]{:T(128)}, /*index=5*/s32[]{:T(128)}, ...), condition=%wide.region_9.10_spmd.clone, body=%wide.region_8.9_spmd.clone.sunk | while | flops 786948 | bytes 271463 | solution.py:152
  157.7 8.0 %all-gather.6 = f32[4,1,256]{2,1,0:T(1,128)S(1)} all-gather(f32[1,1,256]{2,1,0:T(1,128)S(1)} %bitcast.222), channel_id=4, replica_groups=mesh['inner'=4,'outer'=8] {'inner'}, dimensions={0}, use_global_device_ids=true | all-gather | bytes 5120 | tf_op jit(solution)/shard_map/all_gather | solution.py:85
  165.8 1.1 while.133
  166.9 22.8 %all-gather.7 = f32[8,1,256]{2,1,0:T(1,128)S(1)} all-gather(f32[1,1,256]{2,1,0:T(1,128)S(1)} %bitcast.221), channel_id=5, replica_groups=mesh['inner'=4,'outer'=8] {'outer'}, dimensions={0}, use_global_device_ids=true | all-gather | bytes 9216 | tf_op jit(solution)/shard_map/all_gather | solution.py:105
  189.7 12.2 %while.134 = (s32[]{:T(128)}, f32[256]{0:T(256)S(1)}, f32[256]{0:T(256)S(1)}, f32[256,256]{1,0:T(8,128)S(1)}, f32[8,256]{1,0:T(8,128)S(1)}, /*index=5*/s32[8]{0:...) while((s32[]{:T(128)}, f32[256]{0:T(256)S(1)}, f32[256]{0:T(256)S(1)}, ...), condition=%wide.region_13.14_spmd.clone, body=%wide.region_12.13_spmd.clone.sunk | while | flops 787461 | bytes 273557 | solution.py:106
  201.9 6.0 %while.129 = (s32[]{:T(128)}, f32[256]{0:T(256)S(1)}, f32[256]{0:T(256)S(1)}, f32[256,256]{1,0:T(8,128)S(1)}, f32[4,256]{1,0:T(4,128)S(1)}, /*index=5*/s32[4]{0:T(128)S(1)}, s32[]{:T(128)}, s32[]{:T(128)}, s32[]{:T(128)}) while((s32[]{:T(128)}, f32[256]{0:T(256)S(1)}, f32[256]{0:T(256)S(1)}, f32[256,256]{1,0:T(8,128)S(1)}, ...), condition=%wide.region_15.16_spmd, body=%wide.region_14.15_spmd.sunk | while | flops 786948 | bytes 272515 | solution.py:112
  207.9 6.3 %while.130 = (s32[]{:T(128)}, f32[256]{0:T(256)S(1)}, f32[16,256]{1,0:T(8,128)S(1)}, f32[256,256]{1,0:T(8,128)S(1)}, f32[16,256]{1,0:T(8,128)S(1)}, /*index=5*/s32[]{:T(128)}, s32[]{:T(128)}, s32[]{:T(128)}) while((s32[]{:T(128)}, f32[256]{0:T(256)S(1)}, f32[16,256]{1,0:T(8,128)S(1)}, f32[256,256]{1,0:T(8,128)S(1)}, ...), condition=%wide.region_17.18_spmd, body=%wide.region_16.17_spmd.sunk | while | flops 786691 | bytes 271465 | solution.py:155
  (384 shorter events, 59.8 us)
Async XLA Ops:
  7.2 110.5 %copy-start = (f32[256]{0:T(256)S(1)}, f32[256]{0:T(256)}, u32[]{:S(2)}) copy-start(f32[256]{0:T(256)} %param.27) | copy-start | bytes 3076
  7.2 65.9 %all-gather.11.cloned.1.call-start = ((), (), s32[]{:S(2)}) async-start(), calls=%async_computation | async-start | bytes 1351680 | tf_op jit(solution)/shard_map/all_gather | solution.py:58
  42.7 0.7 copy-start.3
  43.4 74.2 %all-gather.13.cloned.1.call-start = ((), (), s32[]{:S(2)}) async-start(), calls=%async_computation.1 | async-start | bytes 2433024 | tf_op jit(solution)/shard_map/all_gather | solution.py:11
  73.1 14.8 %copy-start.1 = (f32[256,256]{1,0:T(8,128)S(1)}, f32[256,256]{1,0:T(8,128)}, u32[]{:S(2)}) copy-start(f32[256,256]{1,0:T(8,128)} %param.26) | copy-start | bytes 786436
  87.1 0.7 copy-start.2
  117.6 0.7 copy-start.4
  151.6 38.1 %copy-start.5 = (f32[16,256]{1,0:T(8,128)}, f32[16,256]{1,0:T(8,128)S(1)}, u32[]{:S(2)}) copy-start(f32[16,256]{1,0:T(8,128)S(1)} %get-tuple-element.684) | copy-start | bytes 49156
Sparse Core Ops, SparseCore 0:
  43.5 29.4 all-gather.10
  87.9 29.6 all-gather.12
where the time goes:
time: 225 us; the launch traced here: 222 us
  matrix products  62.5 us (28%)
  waiting for transfers between devices  56.2 us (25%)
  blocking collectives  30.9 us (14%)
  local copies, waits for them, and re-layouts  30.6 us (14%)
  between operations  14.4 us (6%)
  other arithmetic  14.1 us (6%)
  loops' own time  13 us (6%)
    all_gather x1, waiting for transfers between devices, incoming_state(): gathered = lax.all_gather(own_map[None], 'inner', axis=0, tiled=True)  29.5 us
    all_gather x1, waiting for transfers between devices, entering(): gathered = lax.all_gather(part, axis)  26.7 us
    all_gather x1, blocking collectives, entering_backward(): lax.all_gather(group_offset[None], 'outer', axis=0, tiled=True)  22.8 us
    dot_general x16, matrix products, compose_forward(): lax.dot_general(packed, step_matrix, (((1,), (1,)), ((), ())), precision=...  21.9 us
    dot_general x16, matrix products, forward(): predicted = jnp.dot(step_matrix, state, precision=HIGHEST)  19.5 us
    dynamic_slice x48, local copies, waits for them, and re-layouts, shards(): lax.scan(compose_forward, identity_map(state_width), (jac, obs))  13.3 us
    mul x16, other arithmetic, compose_forward(): return (moved + bottom * (gain_filter * measured)[None, :], None)  11.6 us
    dot_general x32, matrix products, backward(): renewed = jnp.dot(gain_smooth, state, precision=HIGHEST) + term  8.65 us
  transfers between devices with their start and end apart: 2, of which 2 were waited for; matrix products, arithmetic and copies ran while one was open for 1% of the time, Pallas kernels for 0%

commit v1 on v0

--- a/solution.py
+++ b/solution.py
@@ -55,7 +55,15 @@
     identity = identity_map(state_width)
     inner_count = lax.axis_size("inner")
     inner_here = lax.axis_index("inner")
-    gathered = lax.all_gather(own_map[None], "inner", axis=0, tiled=True)
+    ways, here_2 = (lax.axis_size("inner"), lax.axis_index("inner"))
+    grown, reach = (own_map[None], 1)
+    while reach < ways:
+        theirs = lax.ppermute(grown, "inner", [(d, d ^ reach) for d in range(ways)])
+        mine_first = jnp.concatenate([grown, theirs], axis=0)
+        theirs_first = jnp.concatenate([theirs, grown], axis=0)
+        grown = jnp.where(here_2 & reach == 0, mine_first, theirs_first)
+        reach = 2 * reach
+    gathered = grown
 
     def absorb(running, inputs):
         before, group_total = running

time: 225 us -> 214 us (0.951)
  waiting for transfers between devices: 56.2 us -> 45.5 us
  starting transfers between devices: 0.08 us -> 4.9 us
  matrix products: 62.5 us -> 58.7 us
  local copies, waits for them, and re-layouts: 30.6 us -> 28.2 us
    all_gather x1 -> x0, waiting for transfers between devices: 29.5 us -> none  [incoming_state(): gathered = lax.all_gather(own_map[None], 'inner', axis=0, tiled=True)]
    ppermute x0 -> x2, waiting for transfers between devices: none -> 17.6 us  [incoming_state(): theirs = lax.ppermute(grown, 'inner', [(d, d ^ reach) for d in range(ways)])]
    ppermute x0 -> x2, starting transfers between devices: none -> 4.86 us  [incoming_state(): theirs = lax.ppermute(grown, 'inner', [(d, d ^ reach) for d in range(ways)])]
    dot_general x4, matrix products: 5.96 us -> 2.2 us  [compose(): product = jnp.dot(earlier, later[:state_width], precision=HIGHEST)]
    slice x4, local copies, waits for them, and re-layouts: 2.85 us -> 0.04 us  [compose(): return product + last_row(state_width) * later[state_width][None, :]]
  transfers between devices with their start and end apart: 2 -> 3, of which waited for: 2 -> 3; matrix products, arithmetic and copies ran while one was open for 1% -> 1% of each run, Pallas kernels for 0% -> 0%
where the time goes in v1:
time: 214 us; the launch traced here: 211 us
  matrix products  58.7 us (27%)
  waiting for transfers between devices  45.5 us (21%)
  blocking collectives  30.9 us (14%)
  local copies, waits for them, and re-layouts  28.2 us (13%)
  other arithmetic  15.6 us (7%)
  between operations  14.4 us (7%)
  loops' own time  13.1 us (6%)
  starting transfers between devices  4.9 us (2%)
    all_gather x1, waiting for transfers between devices, entering(): gathered = lax.all_gather(part, axis)  27.9 us
    all_gather x1, blocking collectives, entering_backward(): lax.all_gather(group_offset[None], 'outer', axis=0, tiled=True)  22.8 us
    dot_general x16, matrix products, compose_forward(): lax.dot_general(packed, step_matrix, (((1,), (1,)), ((), ())), precision=...  21.9 us
    dot_general x16, matrix products, forward(): predicted = jnp.dot(step_matrix, state, precision=HIGHEST)  19.5 us
    ppermute x2, waiting for transfers between devices, incoming_state(): theirs = lax.ppermute(grown, 'inner', [(d, d ^ reach) for d in range(ways)])  17.6 us
    dynamic_slice x48, local copies, waits for them, and re-layouts, shards(): lax.scan(compose_forward, identity_map(state_width), (jac, obs))  13.3 us
    mul x16, other arithmetic, compose_forward(): return (moved + bottom * (gain_filter * measured)[None, :], None)  11.6 us
    dot_general x32, matrix products, backward(): renewed = jnp.dot(gain_smooth, state, precision=HIGHEST) + term  8.65 us
  transfers between devices with their start and end apart: 3, of which 3 were waited for; matrix products, arithmetic and copies ran while one was open for 1% of the time, Pallas kernels for 0%

profile of v1, /device:TPU:0, one launch (start us, length us, event | category | flops | bytes accessed | tf_op | source)
XLA Modules:
  0.0 211.4 jit_solution(3441077741526511450)
XLA Ops:
  8.0 34.6 %while.131 = (s32[]{:T(128)}, f32[257,256]{1,0:T(8,128)S(1)}, f32[16,256,256]{2,1,0:T(8,128)}, f32[256]{0:T(256)S(1)}, f32[256]{0:T(256)}, /*index=5*/f32[16,256]{1,0:T(8,128)}, s32[]{:T(128)}) while((s32[]{:T(128)}, f32[257,256]{1,0:T(8,128)S(1)}, f32[16,256,256]{2,1,0:T(8,128)}, f32[256]{0:T(256)S(1)}, f32[256]{0:T(256)}, ...), condition=%wide.region_1.2_spmd.clone, body=%wide.region_0.1_spmd.clone.sunk | while | flops 202311168 | bytes 1322585 | solution.py:143
  8.8 1.4 fusion.108
  11.0 1.4 fusion.108
  13.1 1.4 fusion.108
  15.3 1.4 fusion.108
  17.5 1.4 fusion.108
  19.6 1.4 fusion.108
  21.8 1.4 fusion.108
  24.0 1.4 fusion.108
  26.1 1.4 fusion.108
  28.3 1.4 fusion.108
  30.5 1.4 fusion.108
  32.6 1.4 fusion.108
  34.8 1.4 fusion.108
  37.0 1.4 fusion.108
  39.1 1.4 fusion.108
  41.3 1.4 fusion.108
  42.9 3.0 %collective-permute-start = (f32[1,257,256]{2,0,1:T(1,128)S(1)}, f32[1,257,256]{2,0,1:T(1,128)S(1)}, u32[]{:S(2)}, u32[]{:S(2)}) collective-permute-start(f32[1,257,256]{2,0,1:T(1,128)S(1)} %broadcast_in_dim.30), channel_id=1, source_target_pairs={{0,8},{8,0},{16,24},{24,16},{1,9},{9,1},{17,25},{25,17},{2,10},{10... | collective-permute-start | bytes 789512 | tf_op jit(solution)/shard_map/ppermute | solution.py:61
  45.9 6.3 %collective-permute-done = f32[1,257,256]{2,0,1:T(1,128)S(1)} collective-permute-done((f32[1,257,256]{2,0,1:T(1,128)S(1)}, f32[1,257,256]{2,0,1:T(1,128)S(1)}, u32[]{:S(2)}, u32[]{:S(2)}) %collective-permute-start) | collective-permute-done | bytes 263200 | tf_op jit(solution)/shard_map/ppermute | solution.py:61
  53.0 1.8 collective-permute-start.1
  54.9 11.3 %collective-permute-done.1 = f32[2,257,256]{2,0,1:T(2,128)S(1)} collective-permute-done((f32[2,257,256]{2,0,1:T(2,128)S(1)}, f32[2,257,256]{2,0,1:T(2,128)S(1)}, u32[]{:S(2)}, u32[]{:S(2)}) %collective-permute-start.1) | collective-permute-done | bytes 526368 | tf_op jit(solution)/shard_map/ppermute | solution.py:61
  67.0 8.4 %while.126 = (s32[]{:T(128)}, f32[257,256]{1,0:T(8,128)S(1)}, f32[257,256]{1,0:T(8,128)S(1)}, s32[4]{0:T(128)S(1)}, s32[]{:T(128)}, /*index=5*/f32[4,257,256]{2,0,1:T(4,128)S(1)}, s32[]{:T(128)}, s32[]{:T(128)}, s32[]{}) while((s32[]{:T(128)}, f32[257,256]{1,0:T(8,128)S(1)}, f32[257,256]{1,0:T(8,128)S(1)}, s32[4]{0:T(128)S(1)}, s32[]{:T(128)}, ...), condition=%wide.region_3.4_spmd, body=%wide.region_2.3_spmd.sunk | while | flops 202310912 | bytes 2370707 | solution.py:76
  79.4 27.9 %all-gather.8.cloned.1.call-done = f32[8,257,256]{2,1,0:T(8,128)} async-done(((f32[1,257,256]{2,1,0:T(8,128)}), f32[8,257,256]{2,1,0:T(8,128)}) %all-gather.8.cloned.1.call-update) | async-done | bytes 2105360 | tf_op jit(solution)/shard_map/all_gather | solution.py:11
  107.9 33.3 %while.128 = (s32[]{:T(128)}, f32[256]{0:T(256)S(1)}, f32[16,256]{1,0:T(8,128)S(1)}, f32[16,256]{1,0:T(8,128)S(1)}, f32[16,256,256]{2,1,0:T(8,128)}, /*index=5*/...) while((s32[]{:T(128)}, f32[256]{0:T(256)S(1)}, f32[16,256]{1,0:T(8,128)S(1)}, ...), condition=%wide.region_7.8_spmd, body=%wide.region_6.7_spmd.sunk | while | flops 787202 | bytes 275049 | solution.py:152
  107.9 1.2 fusion.98
  109.1 0.8 constant_dynamic-slice_fusion.21
  110.0 1.2 fusion.98
  112.1 1.2 fusion.98
  114.2 1.2 fusion.98
  116.2 1.2 fusion.98
  118.3 1.2 fusion.98
  120.4 1.2 fusion.98
  122.5 1.2 fusion.98
  124.6 1.2 fusion.98
  126.6 1.2 fusion.98
  128.7 1.2 fusion.98
  130.8 1.2 fusion.98
  132.9 1.2 fusion.98
  135.0 1.2 fusion.98
  137.1 1.2 fusion.98
  139.1 1.2 fusion.98
  141.2 6.1 %while.132 = (s32[]{:T(128)}, f32[256]{0:T(256)S(1)}, f32[256,256]{1,0:T(8,128)S(1)}, f32[16,256]{1,0:T(8,128)S(1)}, s32[]{:T(128)}, /*index=5*/s32[]{:T(128)}, s32[]{:T(128)}) while((s32[]{:T(128)}, f32[256]{0:T(256)S(1)}, f32[256,256]{1,0:T(8,128)S(1)}, f32[16,256]{1,0:T(8,128)S(1)}, s32[]{:T(128)}, /*index=5*/s32[]{:T(128)}, ...), condition=%wide.region_9.10_spmd.clone, body=%wide.region_8.9_spmd.clone.sunk | while | flops 786948 | bytes 271463 | solution.py:160
  147.3 8.0 %all-gather.4 = f32[4,1,256]{2,1,0:T(1,128)S(1)} all-gather(f32[1,1,256]{2,1,0:T(1,128)S(1)} %bitcast.222), channel_id=3, replica_groups=mesh['inner'=4,'outer'=8] {'inner'}, dimensions={0}, use_global_device_ids=true | all-gather | bytes 5120 | tf_op jit(solution)/shard_map/all_gather | solution.py:93
  155.4 1.1 while.133
  156.5 22.8 %all-gather.5 = f32[8,1,256]{2,1,0:T(1,128)S(1)} all-gather(f32[1,1,256]{2,1,0:T(1,128)S(1)} %bitcast.221), channel_id=4, replica_groups=mesh['inner'=4,'outer'=8] {'outer'}, dimensions={0}, use_global_device_ids=true | all-gather | bytes 9216 | tf_op jit(solution)/shard_map/all_gather | solution.py:113
  179.3 12.2 %while.134 = (s32[]{:T(128)}, f32[256]{0:T(256)S(1)}, f32[256]{0:T(256)S(1)}, f32[256,256]{1,0:T(8,128)S(1)}, f32[8,256]{1,0:T(8,128)S(1)}, /*index=5*/s32[8]{0:...) while((s32[]{:T(128)}, f32[256]{0:T(256)S(1)}, f32[256]{0:T(256)S(1)}, ...), condition=%wide.region_13.14_spmd.clone, body=%wide.region_12.13_spmd.clone.sunk | while | flops 787461 | bytes 273557 | solution.py:114
  191.5 6.0 %while.129 = (s32[]{:T(128)}, f32[256]{0:T(256)S(1)}, f32[256]{0:T(256)S(1)}, f32[256,256]{1,0:T(8,128)S(1)}, f32[4,256]{1,0:T(4,128)S(1)}, /*index=5*/s32[4]{0:T(128)S(1)}, s32[]{:T(128)}, s32[]{:T(128)}, s32[]{:T(128)}) while((s32[]{:T(128)}, f32[256]{0:T(256)S(1)}, f32[256]{0:T(256)S(1)}, f32[256,256]{1,0:T(8,128)S(1)}, ...), condition=%wide.region_15.16_spmd, body=%wide.region_14.15_spmd.sunk | while | flops 786948 | bytes 272515 | solution.py:120
  197.5 6.4 %while.130 = (s32[]{:T(128)}, f32[256]{0:T(256)S(1)}, f32[16,256]{1,0:T(8,128)S(1)}, f32[256,256]{1,0:T(8,128)S(1)}, f32[16,256]{1,0:T(8,128)S(1)}, /*index=5*/s32[]{:T(128)}, s32[]{:T(128)}, s32[]{:T(128)}) while((s32[]{:T(128)}, f32[256]{0:T(256)S(1)}, f32[16,256]{1,0:T(8,128)S(1)}, f32[256,256]{1,0:T(8,128)S(1)}, ...), condition=%wide.region_17.18_spmd, body=%wide.region_16.17_spmd.sunk | while | flops 786691 | bytes 271465 | solution.py:163
  (395 shorter events, 60.4 us)
Async XLA Ops:
  7.2 100.1 %copy-start = (f32[256]{0:T(256)S(1)}, f32[256]{0:T(256)}, u32[]{:S(2)}) copy-start(f32[256]{0:T(256)} %param.27) | copy-start | bytes 3076
  7.2 100.0 %all-gather.8.cloned.1.call-start = ((), (), s32[]{:S(2)}) async-start(), calls=%async_computation | async-start | bytes 2433024 | tf_op jit(solution)/shard_map/all_gather | solution.py:11
  7.3 47.6 %copy-start.2 = (f32[257,256]{1,0:T(8,128)}, f32[257,256]{1,0:T(8,128)S(1)}, u32[]{:S(2)}) copy-start(f32[257,256]{1,0:T(8,128)S(1)} %pad_convert_fusion) | copy-start | bytes 789508
  42.9 9.4 %collective-permute-start = (f32[1,257,256]{2,0,1:T(1,128)S(1)}, f32[1,257,256]{2,0,1:T(1,128)S(1)}, u32[]{:S(2)}, u32[]{:S(2)}) collective-permute-start(f32[1,257,256]{2,0,1:T(1,128)S(1)} %broadcast_in_dim.30), channel_id=1, source_target_pairs={{0,8},{8,0},{16,24},{24,16},{1,9},{9,1},{17,25},{25,17},{2,10},{10... | collective-permute-start | bytes 789512 | tf_op jit(solution)/shard_map/ppermute | solution.py:61
  53.0 13.2 %collective-permute-start.1 = (f32[2,257,256]{2,0,1:T(2,128)S(1)}, f32[2,257,256]{2,0,1:T(2,128)S(1)}, u32[]{:S(2)}, u32[]{:S(2)}) collective-permute-start(f32[2,257,256]{2,0,1:T(2,128)S(1)} %maximum_select_fusion.1), channel_id=1, source_target_pairs={{0,16},{8,24},{16,0},{24,8},{1,17},{9,25},{17,1},{25,9},{2,18},{10... | collective-permute-start | bytes 1579016 | tf_op jit(solution)/shard_map/ppermute | solution.py:61
  54.9 12.1 %copy-start.5 = (f32[257,256]{1,0:T(8,128)S(1)}, f32[257,256]{1,0:T(8,128)}, u32[]{:S(2)}) copy-start(f32[257,256]{1,0:T(8,128)} %copy-done.2) | copy-start | bytes 789508
  67.0 9.2 %copy-start.1 = (f32[256,256]{1,0:T(8,128)S(1)}, f32[256,256]{1,0:T(8,128)}, u32[]{:S(2)}) copy-start(f32[256,256]{1,0:T(8,128)} %param.26) | copy-start | bytes 786436
  75.4 0.7 copy-start.4
  78.3 29.0 %copy-start.3 = (f32[257,256]{1,0:T(8,128)S(1)}, f32[257,256]{1,0:T(8,128)}, u32[]{:S(2)}) copy-start(f32[257,256]{1,0:T(8,128)} %copy-done.2) | copy-start | bytes 789508
  107.2 0.7 copy-start.6
  141.2 14.1 %copy-start.7 = (f32[16,256]{1,0:T(8,128)}, f32[16,256]{1,0:T(8,128)S(1)}, u32[]{:S(2)}) copy-start(f32[16,256]{1,0:T(8,128)S(1)} %get-tuple-element.684) | copy-start | bytes 49156
Sparse Core Ops, SparseCore 0:
  76.3 30.9 all-gather.7
